TPU v7x, 512 devices: a whole 4x8x8 slice. The times are simulated.
512 devices in a mesh: seq: 128 (over z, y, core), tp: 4 (over x).
Axes of the slice: x: 4, y: 8, z: 8, core: 2. Of those that a mesh axis runs over, the one named last changes fastest.
Arguments:
- queries: bfloat16 [32768, 4096], P('seq', 'tp'), may hold values from -6 to 6, as said below
- keys: bfloat16 [32768, 512], P('seq', 'tp'), may hold values from -6 to 6, as said below
- values: bfloat16 [32768, 512], P('seq', 'tp'), may hold values from -6 to 6
- segment: int32 [32768], P('seq'), may hold values from 0 to 255, never falling along the last dimension, each value on 1 to 512 neighbouring positions
- repack: int32 [32768], P('seq'), may hold values from 0 to 32767, as said below
- proj: bfloat16 [1536, 4096], P('seq', 'tp'), may hold values from -0.5 to 0.5
- student_states: bfloat16 [32768, 1536], P('seq'), may hold values from -6 to 6
- target_row: int32 [32768], P('seq'), may hold values from 0 to 255
Outputs:
- student_rows: bfloat16 [32768, 1536], P('seq', 'tp')
- grad: float32 [1536, 4096], P('seq', 'tp')
Inputs may be any that keep to these rules, and one draw needn't show every extreme that they name: `queries`: scaled normal entries. `keys`: scaled normal entries. `repack`: A permutation of the student rows. Each device's teacher rows go in consecutive groups of 4 rows, in order, each group to one student owner (the device holding student rows owner * 256 to owner * 256 + 255); every device sends exactly 4 rows to each of 64 other devices and none to itself, so at most 4 rows from one device to one owner, reached by every sending pair.
All inputs are finite; a program needn't handle non-finite values.
Results may differ from a plain program's by a relative error of at most 0.0056.
Values may be sent and summed in bfloat16 or wider, within the bound.
No kernel may reach another device: no remote copies, remote signals or barrier semaphores. Data moves between devices by JAX's collectives and lax.ppermute only.
A program may use at most 64 MiB of HBM per device.

v0:
```python
import math
import jax
import jax.numpy as jnp
from jax import lax
from jax.sharding import PartitionSpec as P

HEADS = 32
KV_HEADS = 4
HEAD_DIM = 128
SW = 1536
REACH = 2
GROUP_ROWS = 4
neg_large = -1e30


def passed_along(block, axis, distance):
    devices = range(lax.axis_size(axis))
    route = [(i - distance, i) for i in devices if i - distance in devices]
    return lax.ppermute(block, axis, route)


def attend(queries, keys, values, segment):
    row_count = queries.shape[0]
    lanes = keys.shape[1]
    seg_rows = (segment + 1).astype(jnp.bfloat16).reshape(-1, lanes)
    seg_rows = jnp.concatenate([seg_rows, jnp.zeros((14, lanes), jnp.bfloat16)], 0)
    packed = jnp.concatenate([keys, values, seg_rows], 0)
    blocks = [packed]
    for step in range(1, REACH + 1):
        blocks.insert(0, passed_along(packed, "seq", step))
    all_keys = jnp.concatenate([b[:row_count] for b in blocks], 0)
    all_values = jnp.concatenate([b[row_count : 2 * row_count] for b in blocks], 0)
    key_seg = jnp.concatenate(
        [b[2 * row_count : 2 * row_count + 2].reshape(-1) for b in blocks], 0
    ).astype(jnp.int32)
    key_pos = jnp.arange(3 * row_count, dtype=jnp.int32) - REACH * row_count
    row_pos = jnp.arange(row_count, dtype=jnp.int32)
    allowed = (key_seg[None, :] == (segment + 1)[:, None]) & (key_pos[None, :] <= row_pos[:, None])
    group = HEADS // KV_HEADS
    q_heads = queries.reshape(row_count, group, HEAD_DIM)
    scale = 1.0 / math.sqrt(HEAD_DIM)
    outputs = []
    for head in range(group):
        scores = (
            jnp.einsum("td,sd->ts", q_heads[:, head], all_keys, preferred_element_type=jnp.float32)
            * scale
        )
        scores = jnp.where(allowed, scores, neg_large)
        top = jnp.max(scores, axis=-1, keepdims=True)
        expo = jnp.exp(scores - top)
        weights = (expo / jnp.sum(expo, axis=-1, keepdims=True)).astype(jnp.bfloat16)
        mixed = jnp.einsum("ts,sd->td", weights, all_values, preferred_element_type=jnp.float32)
        outputs.append(mixed.astype(jnp.bfloat16))
    return jnp.concatenate(outputs, axis=1)


def on_device(queries, keys, values, segment, repack, proj, student_states, target_row):
    row_count = queries.shape[0]
    devices = lax.axis_size("seq")
    groups = row_count // GROUP_ROWS
    attended = attend(queries, keys, values, segment)
    target_dev = repack // row_count
    local_slot = repack - target_dev * row_count
    owners = target_dev.reshape(groups, GROUP_ROWS)[:, 0]
    owner_hot = owners[None, :] == jnp.arange(devices, dtype=jnp.int32)[:, None]
    slots_by_group = local_slot.reshape(groups, GROUP_ROWS)
    slot_table = jnp.sum(jnp.where(owner_hot[:, :, None], slots_by_group[None], 0), axis=1)
    slot_table = jnp.where(jnp.any(owner_hot, axis=1)[:, None], slot_table, row_count)
    slots = lax.all_to_all(slot_table, "seq", split_axis=0, concat_axis=0, tiled=True)
    width_share = SW // lax.axis_size("tp")
    tp_index = lax.axis_index("tp")
    targets = student_states[target_row]
    bucket_dev = jnp.arange(devices * GROUP_ROWS, dtype=jnp.int32) // GROUP_ROWS
    bucket_pos = jnp.arange(devices * GROUP_ROWS, dtype=jnp.int32) % GROUP_ROWS
    row_ids = jnp.arange(row_count, dtype=jnp.int32)
    pick = (
        (bucket_dev[:, None] == target_dev[None, :])
        & (bucket_pos[:, None] == (row_ids % GROUP_ROWS)[None, :])
    ).astype(jnp.bfloat16)
    buckets = jnp.dot(pick, attended, preferred_element_type=jnp.float32).astype(jnp.bfloat16)
    arrived = lax.all_to_all(buckets, "seq", split_axis=0, concat_axis=0, tiled=True)
    place = (row_ids[:, None] == slots.reshape(-1)[None, :]).astype(jnp.bfloat16)
    student_x = jnp.dot(place, arrived, preferred_element_type=jnp.float32).astype(jnp.bfloat16)
    all_proj = lax.all_gather(proj, "seq", axis=0, tiled=True)
    y_part = jnp.einsum("tf,nf->tn", student_x, all_proj, preferred_element_type=jnp.float32)
    y_total = lax.psum(y_part, "tp")
    y_rounded = y_total.astype(jnp.bfloat16)
    delta = (y_rounded.astype(jnp.float32) - targets.astype(jnp.float32)).astype(jnp.bfloat16)
    out_rows = lax.dynamic_slice_in_dim(y_rounded, tp_index * width_share, width_share, 1)
    norm_factor = 1.0 / math.sqrt(row_count * devices)
    grad_rows = delta.shape[1] // devices
    term = jnp.einsum("ts,tf->sf", delta, student_x, preferred_element_type=jnp.float32)
    pieces = term.reshape(devices, grad_rows, term.shape[1])
    summed = lax.all_to_all(
        pieces.astype(jnp.bfloat16), "seq", split_axis=0, concat_axis=0, tiled=True
    ).astype(pieces.dtype)
    grad = jnp.sum(summed, axis=0) * norm_factor
    return (out_rows, grad)


def solution(mesh):
    placed = (
        P("seq", "tp"),
        P("seq", "tp"),
        P("seq", "tp"),
        P("seq"),
        P("seq"),
        P("seq", "tp"),
        P("seq", None),
        P("seq"),
    )
    return jax.shard_map(
        on_device,
        mesh=mesh,
        in_specs=placed,
        out_specs=(P("seq", "tp"), P("seq", "tp")),
        check_vma=False,
    )
```

profile of v0, /device:TPU:41, one launch (start us, length us, event | category | flops | bytes accessed | tf_op | source)
XLA Modules:
  0.0 316.8 jit_solution(7449039841433495899)
XLA Ops:
  7.2 0.8 broadcast_add_fusion
  8.0 1.0 maximum_maximum_fusion
  9.1 2.9 collective-permute-start.1
  11.9 2.3 collective-permute-start
  14.2 0.7 multiply_subtract_fusion
  15.6 0.7 copy.29
  16.3 16.6 %all-to-all-start = ((s32[128,1,4]{2,1,0:T(1,128)}), s32[128,1,4]{2,1,0:T(1,128)S(1)}, u32[]{:S(2)}, u32[]{:S(2)}) async-start(s32[128,1,4]{2,1,0:T(1,128)} %copy.29), calls=%async_computation | async-start | bytes 131072 | tf_op jit(solution)/shard_map/all_to_all | solution.py:69
  33.0 0.7 all-gather.3.cloned.1.call-update
  33.7 1.2 copy.30
  35.1 1.2 fusion.52
  36.3 0.3 fusion.53
  36.6 0.3 fusion.54
  37.0 0.4 fusion.55
  38.0 0.3 fusion.56
  38.4 0.2 fusion.29
  38.5 0.4 fusion.57
  39.1 0.3 fusion.58
  39.4 0.2 fusion.31
  39.6 0.3 fusion.59
  40.0 0.2 fusion.32
  40.1 0.3 fusion.16
  40.4 0.3 fusion.17
  40.7 0.3 fusion.18
  41.0 0.3 fusion.19
  41.3 0.3 fusion.20
  41.6 0.3 fusion.21
  41.9 0.3 fusion.22
  42.2 0.3 fusion.23
  42.6 0.5 convolution_convert_fusion.1
  43.0 1.2 all_to_all.16
  44.3 13.7 %all-to-all-start.1 = ((bf16[128,4,1024]{2,1,0:T(4,128)(2,1)}), bf16[128,4,1024]{2,1,0:T(4,128)(2,1)S(1)}, u32[]{:S(2)}, u32[]{:S(2)}) async-start(bf16[128,4,1024]{2,1,0:T(4,128)(2,1)} %all_to_all.16), calls=%async_computation.1 | async-start | bytes 2097152 | tf_op jit(solution)/shard_map/all_to_all | solution.py:81
  58.1 1.3 gather_fusion
  59.4 0.5 broadcast.182
  59.9 0.8 reduce.5
  60.8 26.4 %all-to-all-done.1 = bf16[128,4,1024]{2,1,0:T(4,128)(2,1)S(1)} async-done(((bf16[128,4,1024]{2,1,0:T(4,128)(2,1)}), bf16[128,4,1024]{2,1,0:T(4,128)(2,1)S(1)}, u32[]{:S(2)}, u32[]{:S(2)}) %all-to-all-start.1) | async-done | bytes 1048608 | tf_op jit(solution)/shard_map/all_to_all | solution.py:81
  87.2 1.1 all_to_all.18
  88.3 1.7 convolution_convert_fusion.2
  90.0 46.0 %all-gather.3.cloned.1.call-done = bf16[128,12,1024]{2,1,0:T(8,128)(2,1)} async-done(((bf16[1,12,1024]{2,1,0:T(8,128)(2,1)}), bf16[128,12,1024]{2,1,0:T(8,128)(2,1)}) %all-gather.3.cloned.1.call-update) | async-done | bytes 3145744 | tf_op jit(solution)/shard_map/all_gather | solution.py:84
  136.0 6.2 %reshape.159 = bf16[1536,1024]{1,0:T(8,128)(2,1)} reshape(bf16[128,12,1024]{2,1,0:T(8,128)(2,1)} %all-gather.3.cloned.1.call-done) | data formatting | bytes 6291456
  142.2 4.1 %fusion.60 = f32[256,1536]{1,0:T(8,128)} fusion(bf16[256,1024]{1,0:T(8,128)(2,1)S(1)} %convolution_convert_fusion.2, bf16[1536,1024]{1,0:T(8,128)(2,1)} %reshape.159), kind=kOutput, calls=%fused_computation.134 | convolution fusion | flops 805306368 | bytes 5242880 | tf_op jit(solution)/shard_map/tf,nf->tn/dot_general | solution.py:85
  146.2 33.8 %all-reduce.1 = bf16[256,1536]{1,0:T(8,128)(2,1)S(1)} all-reduce(f32[256,1536]{1,0:T(8,128)} %fusion.60), channel_id=1, replica_groups=mesh['seq'=128,'tp'=4] {'tp'}, use_global_device_ids=true, to_apply=%region_18.19 | all-reduce | flops 393216 | bytes 2359296 | tf_op jit(solution)/shard_map/psum | solution.py:86
  180.0 2.7 convolution_convert_fusion
  182.7 6.1 %convert_element_type.112 = bf16[128,12,1024]{2,1,0:T(8,128)(2,1)} reshape(bf16[1536,1024]{1,0:T(8,128)(2,1)} %convolution_convert_fusion) | data formatting | bytes 6291456 | tf_op jit(solution)/shard_map/convert_element_type | solution.py:95
  188.8 13.8 %all-to-all-start.2 = ((bf16[128,12,1024]{2,1,0:T(8,128)(2,1)}), bf16[128,12,1024]{2,1,0:T(8,128)(2,1)}, u32[]{:S(2)}, u32[]{:S(2)}) async-start(bf16[128,12,1024]{2,1,0:T(8,128)(2,1)} %convert_element_type.112), calls=%async_computation.2 | async-start | bytes 8388608 | tf_op jit(solution)/shard_map/all_to_all | solution.py:94
  202.6 0.7 constant_dynamic-slice_fusion
  203.3 103.0 %all-to-all-done.2 = bf16[128,12,1024]{2,1,0:T(8,128)(2,1)} async-done(((bf16[128,12,1024]{2,1,0:T(8,128)(2,1)}), bf16[128,12,1024]{2,1,0:T(8,128)(2,1)}, u32[]{:S(2)}, u32[]{:S(2)}) %all-to-all-start.2) | async-done | bytes 3145760 | tf_op jit(solution)/shard_map/all_to_all | solution.py:94
  306.3 3.0 convert_reduce_fusion
  309.3 0.6 broadcast_multiply_fusion
  (37 shorter events, 1.8 us)
Async XLA Ops:
  7.2 50.9 %copy-start = (bf16[256,1536]{1,0:T(8,128)(2,1)S(1)}, bf16[256,1536]{1,0:T(8,128)(2,1)}, u32[]{:S(2)}) copy-start(bf16[256,1536]{1,0:T(8,128)(2,1)} %param.14) | copy-start | bytes 2359300
  7.2 29.1 %copy-start.1 = (bf16[256,128]{1,0:T(8,128)(2,1)S(1)}, bf16[256,128]{1,0:T(8,128)(2,1)}, u32[]{:S(2)}) copy-start(bf16[256,128]{1,0:T(8,128)(2,1)} %param.9) | copy-start | bytes 196612
  9.1 25.9 %collective-permute-start.1 = (bf16[528,128]{1,0:T(8,128)(2,1)S(1)}, bf16[528,128]{1,0:T(8,128)(2,1)S(1)}, u32[]{:S(2)}, u32[]{:S(2)}) collective-permute-start(bf16[528,128]{1,0:T(8,128)(2,1)S(1)} %maximum_maximum_fusion), channel_id=1, source_target_pairs={{0,4},{4,8},{8,12},{12,16},{16,20},{20,24},{24,28},{28,32},{32,36}... | collective-permute-start | bytes 405512 | tf_op jit(solution)/shard_map/ppermute | solution.py:19
  11.9 23.1 %collective-permute-start = (bf16[528,128]{1,0:T(8,128)(2,1)S(1)}, bf16[528,128]{1,0:T(8,128)(2,1)S(1)}, u32[]{:S(2)}, u32[]{:S(2)}) collective-permute-start(bf16[528,128]{1,0:T(8,128)(2,1)S(1)} %maximum_maximum_fusion), channel_id=1, source_target_pairs={{0,8},{4,12},{8,16},{12,20},{16,24},{20,28},{24,32},{28,36},{32,40... | collective-permute-start | bytes 405512 | tf_op jit(solution)/shard_map/ppermute | solution.py:19
  16.3 28.0 %all-to-all-start = ((s32[128,1,4]{2,1,0:T(1,128)}), s32[128,1,4]{2,1,0:T(1,128)S(1)}, u32[]{:S(2)}, u32[]{:S(2)}) async-start(s32[128,1,4]{2,1,0:T(1,128)} %copy.29), calls=%async_computation | async-start | bytes 131072 | tf_op jit(solution)/shard_map/all_to_all | solution.py:69
  33.0 103.0 %all-gather.3.cloned.1.call-start = ((), (), s32[]{:S(2)}) async-start(), calls=%async_computation.3 | async-start | bytes 4227072 | tf_op jit(solution)/shard_map/all_gather | solution.py:84
  38.9 1.2 copy-start.2
  42.5 15.5 %copy-start.3 = (s32[256]{0:T(256)S(1)}, s32[256]{0:T(256)}, u32[]{:S(2)}) copy-start(s32[256]{0:T(256)} %param.15) | copy-start | bytes 3076
  44.3 42.9 %all-to-all-start.1 = ((bf16[128,4,1024]{2,1,0:T(4,128)(2,1)}), bf16[128,4,1024]{2,1,0:T(4,128)(2,1)S(1)}, u32[]{:S(2)}, u32[]{:S(2)}) async-start(bf16[128,4,1024]{2,1,0:T(4,128)(2,1)} %all_to_all.16), calls=%async_computation.1 | async-start | bytes 2097152 | tf_op jit(solution)/shard_map/all_to_all | solution.py:81
  188.8 117.5 %all-to-all-start.2 = ((bf16[128,12,1024]{2,1,0:T(8,128)(2,1)}), bf16[128,12,1024]{2,1,0:T(8,128)(2,1)}, u32[]{:S(2)}, u32[]{:S(2)}) async-start(bf16[128,12,1024]{2,1,0:T(8,128)(2,1)} %convert_element_type.112), calls=%async_computation.2 | async-start | bytes 8388608 | tf_op jit(solution)/shard_map/all_to_all | solution.py:94
Sparse Core Ops, SparseCore 0:
  36.9 99.0 all-gather.2
where the time goes:
time: 318 us; the launch traced here: 317 us
  waiting for transfers between devices  176 us (55%)
  starting transfers between devices  49.4 us (16%)
  blocking collectives  33.8 us (11%)
  local copies, waits for them, and re-layouts  19.7 us (6%)
  matrix products  14.9 us (5%)
  between operations  14.4 us (5%)
  other arithmetic  8.56 us (3%)
    all_to_all x1, waiting for transfers between devices, on_device(): lax.all_to_all(pieces.astype(jnp.bfloat16), 'seq', split_axis=0, concat_a...  103 us
    all_gather x1, waiting for transfers between devices, on_device(): all_proj = lax.all_gather(proj, 'seq', axis=0, tiled=True)  46 us
    psum x1, blocking collectives, on_device(): y_total = lax.psum(y_part, 'tp')  33.8 us
    all_to_all x1, waiting for transfers between devices, on_device(): lax.all_to_all(buckets, 'seq', split_axis=0, concat_axis=0, tiled=True)  26.4 us
    all_to_all x1, starting transfers between devices, on_device(): lax.all_to_all(slot_table, 'seq', split_axis=0, concat_axis=0, tiled=True)  16.6 us
    all_to_all x1, starting transfers between devices, on_device(): lax.all_to_all(pieces.astype(jnp.bfloat16), 'seq', split_axis=0, concat_a...  13.8 us
    all_to_all x1, starting transfers between devices, on_device(): lax.all_to_all(buckets, 'seq', split_axis=0, concat_axis=0, tiled=True)  13.7 us
    unnamed x10, local copies, waits for them, and re-layouts  7.43 us
  transfers between devices with their start and end apart: 6, of which 3 were waited for; matrix products, arithmetic and copies ran while one was open for 5% of the time, Pallas kernels for 0%

commit v1 on v0

--- a/solution.py
+++ b/solution.py
@@ -1,3 +1,4 @@
+import functools
 import math
 import jax
 import jax.numpy as jnp
@@ -11,6 +12,15 @@
 REACH = 2
 GROUP_ROWS = 4
 neg_large = -1e30
+
+
+def domain_unite(u_in, axis_id):
+    return jnp.concatenate(
+        lax.all_to_all(jnp.stack([u_in] * lax.psum(1, axis_id)), axis_id, 0, 0), axis=0
+    )
+
+
+check_lines = functools.partial(domain_unite, axis_id="seq")
 
 
 def passed_along(block, axis, distance):
@@ -81,7 +91,7 @@
     arrived = lax.all_to_all(buckets, "seq", split_axis=0, concat_axis=0, tiled=True)
     place = (row_ids[:, None] == slots.reshape(-1)[None, :]).astype(jnp.bfloat16)
     student_x = jnp.dot(place, arrived, preferred_element_type=jnp.float32).astype(jnp.bfloat16)
-    all_proj = lax.all_gather(proj, "seq", axis=0, tiled=True)
+    all_proj = check_lines(proj)
     y_part = jnp.einsum("tf,nf->tn", student_x, all_proj, preferred_element_type=jnp.float32)
     y_total = lax.psum(y_part, "tp")
     y_rounded = y_total.astype(jnp.bfloat16)

time: 318 us -> 369 us (1.16)
  blocking collectives: 33.8 us -> 75.9 us
  waiting for transfers between devices: 176 us -> 198 us
  between operations: 14.4 us -> 0.97 us
    all_to_all x1, waiting for transfers between devices: 26.4 us -> 95.4 us  [domain_unite(): lax.all_to_all(jnp.stack([u_in] * lax.psum(1, axis_id)), axis_id, 0, 0)]
    all_gather x1 -> x0, waiting for transfers between devices: 46 us -> none  [on_device(): all_proj = lax.all_gather(proj, 'seq', axis=0, tiled=True)]
    all_to_all x0 -> x1, blocking collectives: none -> 42.3 us  [on_device(): lax.all_to_all(buckets, 'seq', split_axis=0, concat_axis=0, tiled=True)]
    reshape x0 -> x1, local copies, waits for them, and re-layouts: none -> 6.16 us  [domain_unite(): jnp.concatenate(lax.all_to_all(jnp.stack([u_in] * lax.psum(1, axis_id)),...]
    unnamed x10 -> x11, local copies, waits for them, and re-layouts: 7.43 us -> 1.28 us
    all_to_all x1, starting transfers between devices: 13.7 us -> 9.14 us  [domain_unite(): lax.all_to_all(jnp.stack([u_in] * lax.psum(1, axis_id)), axis_id, 0, 0)]
  transfers between devices with their start and end apart: 6 -> 5, of which waited for: 3 -> 2; matrix products, arithmetic and copies ran while one was open for 5% -> 4% of each run, Pallas kernels for 0% -> 0%
where the time goes in v1:
time: 369 us; the launch traced here: 368 us
  waiting for transfers between devices  198 us (54%)
  blocking collectives  75.9 us (21%)
  starting transfers between devices  47.3 us (13%)
  local copies, waits for them, and re-layouts  21.5 us (6%)
  matrix products  14.9 us (4%)
  other arithmetic  8.56 us (2%)
    all_to_all x1, waiting for transfers between devices, on_device(): lax.all_to_all(pieces.astype(jnp.bfloat16), 'seq', split_axis=0, concat_a...  103 us
    all_to_all x1, waiting for transfers between devices, domain_unite(): lax.all_to_all(jnp.stack([u_in] * lax.psum(1, axis_id)), axis_id, 0, 0)  95.4 us
    all_to_all x1, blocking collectives, on_device(): lax.all_to_all(buckets, 'seq', split_axis=0, concat_axis=0, tiled=True)  42.3 us
    psum x1, blocking collectives, on_device(): y_total = lax.psum(y_part, 'tp')  33.6 us
    all_to_all x1, starting transfers between devices, on_device(): lax.all_to_all(slot_table, 'seq', split_axis=0, concat_axis=0, tiled=True)  16.6 us
    all_to_all x1, starting transfers between devices, on_device(): lax.all_to_all(pieces.astype(jnp.bfloat16), 'seq', split_axis=0, concat_a...  16.4 us
    all_to_all x1, starting transfers between devices, domain_unite(): lax.all_to_all(jnp.stack([u_in] * lax.psum(1, axis_id)), axis_id, 0, 0)  9.14 us
  transfers between devices with their start and end apart: 5, of which 2 were waited for; matrix products, arithmetic and copies ran while one was open for 4% of the time, Pallas kernels for 0%

profile of v1, /device:TPU:41, one launch (start us, length us, event | category | flops | bytes accessed | tf_op | source)
XLA Modules:
  0.0 367.6 jit_solution(6320810882202520364)
XLA Ops:
  0.7 0.8 broadcast_add_fusion
  1.5 1.0 maximum_maximum_fusion
  2.5 2.9 collective-permute-start.1
  5.4 2.3 collective-permute-start
  7.7 0.7 multiply_subtract_fusion
  9.0 0.7 copy.29
  9.8 16.6 %all-to-all-start = ((s32[128,1,4]{2,1,0:T(1,128)}), s32[128,1,4]{2,1,0:T(1,128)S(1)}, u32[]{:S(2)}, u32[]{:S(2)}) async-start(s32[128,1,4]{2,1,0:T(1,128)} %copy.29), calls=%async_computation | async-start | bytes 131072 | tf_op jit(solution)/shard_map/all_to_all | solution.py:79
  26.5 1.2 copy.30
  27.8 1.2 fusion.52
  29.0 0.3 fusion.53
  29.4 0.3 fusion.54
  29.7 0.3 fusion.55
  30.1 0.3 fusion.56
  30.4 0.3 fusion.57
  30.8 0.3 fusion.58
  31.1 0.3 fusion.59
  31.8 0.3 fusion.16
  32.1 0.3 fusion.17
  32.4 0.2 fusion.27
  32.6 0.3 fusion.18
  32.9 0.2 fusion.28
  33.1 0.3 fusion.19
  33.5 0.3 fusion.20
  34.0 0.3 fusion.21
  34.5 0.3 fusion.22
  34.8 0.2 fusion.32
  35.0 0.3 fusion.23
  35.3 0.5 convolution_convert_fusion.1
  35.8 0.4 all_to_all.19
  36.2 42.3 %all_to_all.28 = bf16[128,4,1024]{2,1,0:T(4,128)(2,1)S(1)} all-to-all(bf16[128,4,1024]{2,1,0:T(4,128)(2,1)S(1)} %all_to_all.19), channel_id=1, replica_groups=mesh['seq'=128,'tp'=4] {'seq'}, dimensions={0} | all-to-all | bytes 2097152 | tf_op jit(solution)/shard_map/all_to_all | solution.py:91
  78.5 2.5 stack.2
  81.0 9.1 %all-to-all-start.2 = ((bf16[128,12,1024]{2,1,0:T(8,128)(2,1)}), bf16[128,12,1024]{2,1,0:T(8,128)(2,1)}, u32[]{:S(2)}, u32[]{:S(2)}) async-start(bf16[128,12,1024]{2,1,0:T(8,128)(2,1)} %stack.2), calls=%async_computation.2 | async-start | bytes 8388608 | tf_op jit(solution)/shard_map/all_to_all | solution.py:19
  90.2 1.3 gather_fusion
  91.5 0.5 broadcast.184
  92.0 0.8 reduce.5
  92.9 1.2 all_to_all.21
  94.2 1.7 convolution_convert_fusion.2
  95.8 95.4 %all-to-all-done.2 = bf16[128,12,1024]{2,1,0:T(8,128)(2,1)} async-done(((bf16[128,12,1024]{2,1,0:T(8,128)(2,1)}), bf16[128,12,1024]{2,1,0:T(8,128)(2,1)}, u32[]{:S(2)}, u32[]{:S(2)}) %all-to-all-start.2) | async-done | bytes 3145760 | tf_op jit(solution)/shard_map/all_to_all | solution.py:19
  191.2 6.2 %reshape.154 = bf16[1536,1024]{1,0:T(8,128)(2,1)} reshape(bf16[128,12,1024]{2,1,0:T(8,128)(2,1)} %all-to-all-done.2) | data formatting | bytes 6291456 | tf_op jit(solution)/shard_map/reshape | solution.py:18
  197.4 4.1 %fusion.60 = f32[256,1536]{1,0:T(8,128)} fusion(bf16[256,1024]{1,0:T(8,128)(2,1)S(1)} %convolution_convert_fusion.2, bf16[1536,1024]{1,0:T(8,128)(2,1)} %reshape.154), kind=kOutput, calls=%fused_computation.134 | convolution fusion | flops 805306368 | bytes 5242880 | tf_op jit(solution)/shard_map/tf,nf->tn/dot_general | solution.py:95
  201.4 33.6 %all-reduce.1 = bf16[256,1536]{1,0:T(8,128)(2,1)S(1)} all-reduce(f32[256,1536]{1,0:T(8,128)} %fusion.60), channel_id=1, replica_groups=mesh['seq'=128,'tp'=4] {'tp'}, use_global_device_ids=true, to_apply=%region_18.19 | all-reduce | flops 393216 | bytes 2359296 | tf_op jit(solution)/shard_map/psum | solution.py:96
  235.1 2.7 convolution_convert_fusion
  237.8 6.1 %convert_element_type.112 = bf16[128,12,1024]{2,1,0:T(8,128)(2,1)} reshape(bf16[1536,1024]{1,0:T(8,128)(2,1)} %convolution_convert_fusion) | data formatting | bytes 6291456 | tf_op jit(solution)/shard_map/convert_element_type | solution.py:105
  243.8 16.4 %all-to-all-start.3 = ((bf16[128,12,1024]{2,1,0:T(8,128)(2,1)}), bf16[128,12,1024]{2,1,0:T(8,128)(2,1)}, u32[]{:S(2)}, u32[]{:S(2)}) async-start(bf16[128,12,1024]{2,1,0:T(8,128)(2,1)} %convert_element_type.112), calls=%async_computation.3 | async-start | bytes 8388608 | tf_op jit(solution)/shard_map/all_to_all | solution.py:104
  260.2 0.7 constant_dynamic-slice_fusion
  260.9 103.0 %all-to-all-done.3 = bf16[128,12,1024]{2,1,0:T(8,128)(2,1)} async-done(((bf16[128,12,1024]{2,1,0:T(8,128)(2,1)}), bf16[128,12,1024]{2,1,0:T(8,128)(2,1)}, u32[]{:S(2)}, u32[]{:S(2)}) %all-to-all-start.3) | async-done | bytes 3145760 | tf_op jit(solution)/shard_map/all_to_all | solution.py:104
  363.9 3.0 convert_reduce_fusion
  366.9 0.6 broadcast_multiply_fusion
  (38 shorter events, 1.8 us)
Async XLA Ops:
  0.6 89.6 %copy-start = (bf16[256,1536]{1,0:T(8,128)(2,1)S(1)}, bf16[256,1536]{1,0:T(8,128)(2,1)}, u32[]{:S(2)}) copy-start(bf16[256,1536]{1,0:T(8,128)(2,1)} %param.14) | copy-start | bytes 2359300
  0.6 28.4 %copy-start.1 = (bf16[256,128]{1,0:T(8,128)(2,1)S(1)}, bf16[256,128]{1,0:T(8,128)(2,1)}, u32[]{:S(2)}) copy-start(bf16[256,128]{1,0:T(8,128)(2,1)} %param.9) | copy-start | bytes 196612
  2.5 25.2 %collective-permute-start.1 = (bf16[528,128]{1,0:T(8,128)(2,1)S(1)}, bf16[528,128]{1,0:T(8,128)(2,1)S(1)}, u32[]{:S(2)}, u32[]{:S(2)}) collective-permute-start(bf16[528,128]{1,0:T(8,128)(2,1)S(1)} %maximum_maximum_fusion), channel_id=1, source_target_pairs={{0,4},{4,8},{8,12},{12,16},{16,20},{20,24},{24,28},{28,32},{32,36}... | collective-permute-start | bytes 405512 | tf_op jit(solution)/shard_map/ppermute | solution.py:29
  5.4 22.3 %collective-permute-start = (bf16[528,128]{1,0:T(8,128)(2,1)S(1)}, bf16[528,128]{1,0:T(8,128)(2,1)S(1)}, u32[]{:S(2)}, u32[]{:S(2)}) collective-permute-start(bf16[528,128]{1,0:T(8,128)(2,1)S(1)} %maximum_maximum_fusion), channel_id=1, source_target_pairs={{0,8},{4,12},{8,16},{12,20},{16,24},{20,28},{24,32},{28,36},{32,40... | collective-permute-start | bytes 405512 | tf_op jit(solution)/shard_map/ppermute | solution.py:29
  9.8 26.4 %all-to-all-start = ((s32[128,1,4]{2,1,0:T(1,128)}), s32[128,1,4]{2,1,0:T(1,128)S(1)}, u32[]{:S(2)}, u32[]{:S(2)}) async-start(s32[128,1,4]{2,1,0:T(1,128)} %copy.29), calls=%async_computation | async-start | bytes 131072 | tf_op jit(solution)/shard_map/all_to_all | solution.py:79
  30.8 1.1 copy-start.2
  35.2 43.3 %copy-start.3 = (bf16[12,1024]{1,0:T(8,128)(2,1)S(1)}, bf16[12,1024]{1,0:T(8,128)(2,1)}, u32[]{:S(2)}) copy-start(bf16[12,1024]{1,0:T(8,128)(2,1)} %param.13) | copy-start | bytes 73732
  81.0 9.2 %copy-start.4 = (s32[256]{0:T(256)S(1)}, s32[256]{0:T(256)}, u32[]{:S(2)}) copy-start(s32[256]{0:T(256)} %param.15) | copy-start | bytes 3076
  81.0 110.2 %all-to-all-start.2 = ((bf16[128,12,1024]{2,1,0:T(8,128)(2,1)}), bf16[128,12,1024]{2,1,0:T(8,128)(2,1)}, u32[]{:S(2)}, u32[]{:S(2)}) async-start(bf16[128,12,1024]{2,1,0:T(8,128)(2,1)} %stack.2), calls=%async_computation.2 | async-start | bytes 8388608 | tf_op jit(solution)/shard_map/all_to_all | solution.py:19
  243.8 120.1 %all-to-all-start.3 = ((bf16[128,12,1024]{2,1,0:T(8,128)(2,1)}), bf16[128,12,1024]{2,1,0:T(8,128)(2,1)}, u32[]{:S(2)}, u32[]{:S(2)}) async-start(bf16[128,12,1024]{2,1,0:T(8,128)(2,1)} %convert_element_type.112), calls=%async_computation.3 | async-start | bytes 8388608 | tf_op jit(solution)/shard_map/all_to_all | solution.py:104
